TPU v7x, 256 devices: a whole 4x4x8 slice. The times are simulated.
256 devices in a mesh: tiles: 64 (over y, z, core), rep: 4 (over x).
Axes of the slice: x: 4, y: 4, z: 8, core: 2. Of those that a mesh axis runs over, the one named last changes fastest.
Arguments:
- trailing_tiles: float32 [5120, 256, 256], P(('tiles', 'rep')), may hold values from -6 to 6
- panel_rows: float32 [128, 256, 512], P('tiles'), may hold values from -3 to 3
- pivot_blocks: float32 [2, 256, 256], replicated
- coupling: float32 [256, 256], replicated, may hold values from -0.1875 to 0.1875
- row_ids: int32 [128], replicated, may hold values from 2 to 96, as said below
- membership: int32 [64, 24], replicated, may hold values from 2 to 96, as said below
- tile_pairs: int32 [5120, 2], P(('tiles', 'rep')), may hold values from 0 to 24, as said below
Outputs:
- updated_tiles: float32 [5120, 256, 256], P(('tiles', 'rep'))
- factors: float32 [128, 256, 512], P('tiles')
- pivot_diag: float32 [2, 256], replicated
Inputs may be any that keep to these rules, and one draw needn't show every extreme that they name: `row_ids`: each row block 2 to 95 stands in exactly one slot; the other slots hold 96. `membership`: entries are row blocks 2 to 95, or 96 for none. `tile_pairs`: a slot's first entry is below 12, its second from 12 to 23, or both are 24 for an empty slot; over all devices every unordered pair of row blocks 2 to 96 - 1 (a block with itself too) is listed exactly once; some device fills all 20 slots.
All inputs are finite; a program needn't handle non-finite values.
Results may differ from a plain program's by a relative error of at most 0.00005.
Values sent between devices are 32-bit elements; how exact they have to be, the bound alone decides.
No kernel may reach another device: no remote copies, remote signals or barrier semaphores. Data moves between devices by JAX's collectives and lax.ppermute only.
A program may use at most 128 MiB of HBM per device.

v0:
```python
import jax
import jax.numpy as jnp
from jax import lax
from jax.sharding import PartitionSpec as P

NB = 96


def pivot_factor(matrix):
    lower_factor = jnp.linalg.cholesky(matrix)
    pivots = jnp.diagonal(lower_factor)
    identity = jnp.eye(matrix.shape[0], dtype=matrix.dtype)
    inverse = jax.scipy.linalg.solve_triangular(lower_factor, identity, lower=True)
    return (inverse.T / pivots[None, :], pivots * pivots)


def panel_factors(panel_rows, pivot_blocks, coupling, usable):
    panel_width = pivot_blocks.shape[1]
    solve_one, diag_one = pivot_factor(pivot_blocks[0])
    coupled = jnp.dot(coupling, solve_one, precision=lax.Precision.HIGHEST)
    schur = pivot_blocks[1] - jnp.dot(
        coupled * diag_one[None, :], coupled.T, precision=lax.Precision.HIGHEST
    )
    solve_two, diag_two = pivot_factor(schur)
    first = jnp.einsum(
        "rik,kj->rij", panel_rows[:, :, :panel_width], solve_one, precision=lax.Precision.HIGHEST
    )
    second_raw = panel_rows[:, :, panel_width:] - jnp.einsum(
        "rik,jk->rij", first * diag_one[None, None, :], coupled, precision=lax.Precision.HIGHEST
    )
    second = jnp.einsum("rik,kj->rij", second_raw, solve_two, precision=lax.Precision.HIGHEST)
    joined = jnp.concatenate([first, second], axis=2)
    factors = jnp.where(usable[:, None, None], joined, jnp.zeros_like(joined))
    return (factors, diag_one, diag_two)


def pair_products(group_rows, scales, tile_pairs):
    padding = jnp.zeros((1,) + group_rows.shape[1:], group_rows.dtype)
    extended = jnp.concatenate([group_rows, padding], axis=0)
    left_rows = extended[tile_pairs[:, 0]] * scales[None, None, :]
    right_rows = extended[tile_pairs[:, 1]]
    return jnp.einsum("sik,sjk->sij", left_rows, right_rows, precision=lax.Precision.HIGHEST)


def per_device(trailing_tiles, panel_rows, pivot_blocks, coupling, row_ids, membership, tile_pairs):
    owned_slots = panel_rows.shape[0]
    panel_width = pivot_blocks.shape[1]
    tile_index = lax.axis_index("tiles")
    own_ids = lax.dynamic_slice_in_dim(row_ids, tile_index * owned_slots, owned_slots)
    factors, diag_one, diag_two = panel_factors(panel_rows, pivot_blocks, coupling, own_ids < NB)
    quarter = panel_width // lax.axis_size("rep")
    my_rows = lax.dynamic_slice_in_dim(factors, lax.axis_index("rep") * quarter, quarter, 1)
    wanted = lax.dynamic_index_in_dim(membership, tile_index, 0, keepdims=False)
    picker = (wanted[:, None] == row_ids[None, :]).astype(jnp.float32)
    selected = jnp.einsum(
        "gn,nij->gij",
        picker,
        lax.all_gather(my_rows, "tiles", axis=0, tiled=True),
        precision=lax.Precision.HIGHEST,
    )
    group_rows = lax.all_gather(selected, "rep", axis=1, tiled=True)
    scales = jnp.concatenate([diag_one, diag_two])
    updated = trailing_tiles - pair_products(group_rows, scales, tile_pairs)
    return (updated, factors, jnp.stack([diag_one, diag_two]))


def solution(mesh):
    return jax.shard_map(
        per_device,
        mesh=mesh,
        in_specs=(
            P(("tiles", "rep"), None, None),
            P("tiles", None, None),
            P(),
            P(),
            P(),
            P(),
            P(("tiles", "rep"), None),
        ),
        out_specs=(P(("tiles", "rep"), None, None), P("tiles", None, None), P()),
        check_vma=False,
    )
```

profile of v0, /device:TPU:1, one launch (start us, length us, event | category | flops | bytes accessed | tf_op | source)
XLA Modules:
  0.0 469.8 jit_solution(16418581073908269618)
XLA Ops:
  7.2 0.0 copy-start
  7.2 0.0 all-gather.3.cloned.1.call-start
  7.3 1.1 fusion.52
  8.5 0.1 copy.40
  8.6 1.0 fusion.16
  9.6 11.7 %cholesky.130 = f32[128,128]{1,0:T(8,128)S(1)} custom-call(f32[128,128]{1,0:T(8,128)S(1)} %cholesky.194), custom_call_target="Cholesky" | custom-call | tf_op jit(solution)/shard_map/jit(cholesky)/cholesky | solution.py:10
  21.4 9.8 %custom-call.17 = f32[1,128,128]{1,2,0:T(8,128)S(1)} custom-call(f32[1,128,128]{2,1,0:T(8,128)S(1)} %get-tuple-element.63), custom_call_target="InvertDiagBlocksLowerTriangular" | custom-call | tf_op jit(solution)/shard_map/jit(cholesky)/cholesky | solution.py:10
  31.2 0.2 constant_dynamic-update-slice_fusion.3
  31.4 0.3 convolution_subtract_fusion.5
  31.7 11.7 %cholesky.147 = f32[128,128]{1,0:T(8,128)S(1)} custom-call(f32[128,128]{1,0:T(8,128)S(1)} %convolution_subtract_fusion.5), custom_call_target="Cholesky" | custom-call | tf_op jit(solution)/shard_map/jit(cholesky)/cholesky | solution.py:10
  43.4 0.6 compare_reduce_fusion.2
  45.4 0.1 triangular_solve.75
  45.5 4.2 while.4
  45.7 0.6 fusion.67
  46.3 1.4 bitcast_dynamic-update-slice_fusion.4
  47.8 0.6 fusion.67
  48.3 1.4 bitcast_dynamic-update-slice_fusion.4
  49.7 19.7 %custom-call.18 = f32[2,128,128]{1,2,0:T(8,128)S(1)} custom-call(f32[2,128,128]{2,1,0:T(8,128)S(1)} %get-tuple-element.19), custom_call_target="InvertDiagBlocksLowerTriangular" | custom-call | tf_op jit(solution)/shard_map/jit(_solve_triangular)/triangular_solve | solution.py:13
  69.4 0.3 fusion.29
  69.7 0.3 convolution_subtract_fusion.3
  70.0 0.3 fusion.36
  70.3 2.3 gather_fusion
  72.7 0.1 copy.41
  72.8 0.4 fusion.48
  73.3 0.7 convolution_subtract_fusion.1
  73.9 0.1 copy.33
  74.1 11.7 %cholesky.164 = f32[128,128]{1,0:T(8,128)S(1)} custom-call(f32[128,128]{1,0:T(8,128)S(1)} %cholesky.197), custom_call_target="Cholesky" | custom-call | tf_op jit(solution)/shard_map/jit(cholesky)/cholesky | solution.py:10
  85.9 9.8 %custom-call.19 = f32[1,128,128]{1,2,0:T(8,128)S(1)} custom-call(f32[1,128,128]{2,1,0:T(8,128)S(1)} %get-tuple-element.59), custom_call_target="InvertDiagBlocksLowerTriangular" | custom-call | tf_op jit(solution)/shard_map/jit(cholesky)/cholesky | solution.py:10
  95.7 0.2 constant_dynamic-update-slice_fusion.1
  95.9 0.3 convolution_subtract_fusion.4
  96.2 11.7 %cholesky.181 = f32[128,128]{1,0:T(8,128)S(1)} custom-call(f32[128,128]{1,0:T(8,128)S(1)} %convolution_subtract_fusion.4), custom_call_target="Cholesky" | custom-call | tf_op jit(solution)/shard_map/jit(cholesky)/cholesky | solution.py:10
  107.9 0.6 compare_reduce_fusion
  108.6 0.6 compare_reduce_fusion.1
  110.6 4.0 while.5
  110.6 0.6 fusion.68
  111.2 1.4 bitcast_dynamic-update-slice_fusion.5
  112.6 0.6 fusion.68
  113.2 1.4 bitcast_dynamic-update-slice_fusion.5
  114.6 20.1 %custom-call.20 = f32[2,128,128]{1,2,0:T(8,128)S(1)} custom-call(f32[2,128,128]{2,1,0:T(8,128)S(1)} %get-tuple-element.20), custom_call_target="InvertDiagBlocksLowerTriangular" | custom-call | tf_op jit(solution)/shard_map/jit(_solve_triangular)/triangular_solve | solution.py:13
  134.7 0.3 fusion.27
  135.0 0.3 convolution_subtract_fusion.2
  135.3 0.3 fusion.32
  135.6 2.3 gather_fusion.1
  137.9 0.6 convolution_bitcast_fusion
  138.6 1.1 convolution_subtract_fusion
  139.7 0.1 dynamic-slice_compare_fusion
  139.8 0.6 fusion.12
  140.4 0.1 maximum_select_fusion
  140.6 0.2 constant_dynamic-slice_fusion.2
  140.8 0.9 copy.34
  141.7 0.0 all-gather.3.cloned.1.call-update
  141.7 0.0 all-gather.5.cloned.1.call-start
  141.8 0.2 dynamic-slice_reduce_fusion
  141.9 103.4 %all-gather.3.cloned.1.call-done = f32[128,64,512]{2,1,0:T(8,128)} async-done(((f32[2,64,512]{2,1,0:T(8,128)}), f32[128,64,512]{2,1,0:T(8,128)}) %all-gather.3.cloned.1.call-update) | async-done | bytes 16777232 | tf_op jit(solution)/shard_map/all_gather | solution.py:58
  245.3 21.4 %fusion = f32[24,64,512]{2,0,1:T(8,128)} fusion(f32[128,64,512]{2,1,0:T(8,128)} %all-gather.3.cloned.1.call-done, s32[128]{0:T(128)S(1)} %copy-done.5, s32[24]{0:T(128)S(1)} %dynamic-slice_reduce_fusion), kind=kOutput, calls=%fused_computation.8 | convolution fusion | flops 1207962624 | bytes 19923552 | tf_op jit(solution)/shard_map/gn,nij->gij/dot_general | solution.py:55
  266.7 0.0 all-gather.5.cloned.1.call-update
  266.8 1.3 copy.37
  268.1 0.6 pad_maximum_fusion.1
  268.7 115.7 %all-gather.5.cloned.1.call-done = f32[24,256,512]{2,0,1:T(8,128)} async-done(((f32[24,64,512]{2,0,1:T(8,128)}), f32[24,256,512]{2,0,1:T(8,128)}) %all-gather.5.cloned.1.call-update) | async-done | bytes 12582928 | tf_op jit(solution)/shard_map/all_gather | solution.py:61
  384.4 16.4 %copy.36 = f32[24,256,512]{2,1,0:T(8,128)} copy(f32[24,256,512]{2,0,1:T(8,128)} %all-gather.5.cloned.1.call-done) | data formatting | bytes 25165824 | tf_op jit(solution)/shard_map/all_gather | solution.py:61
  400.8 11.6 %concatenate.18 = f32[25,256,512]{2,1,0:T(8,128)} pad(f32[24,256,512]{2,1,0:T(8,128)} %copy.36, f32[]{:T(128)} %constant.92.clone.1), padding=0_1x0_0x0_0 | pad | bytes 25690116 | tf_op jit(solution)/shard_map/concatenate | solution.py:39
  412.4 11.2 %gather_fusion.2 = f32[20,256,512]{2,1,0:T(8,128)} fusion(f32[25,256,512]{2,1,0:T(8,128)} %concatenate.18, s32[1024]{0:T(1024)S(1)} %get-tuple-element.73), kind=kCustom, calls=%fused_computation.2 | custom fusion | bytes 20971600 | tf_op jit(solution)/shard_map/gather | solution.py:40
  423.5 11.5 %gather_fusion.3 = f32[20,256,512]{2,1,0:T(8,128)} fusion(f32[25,256,512]{2,1,0:T(8,128)} %concatenate.18, s32[1024]{0:T(1024)S(1)} %get-tuple-element.72), kind=kCustom, calls=%fused_computation.3 | custom fusion | bytes 20971600 | tf_op jit(solution)/shard_map/gather | solution.py:41
  435.1 27.4 %fusion.5 = f32[20,256,256]{2,1,0:T(8,128)} fusion(f32[20,256,256]{2,1,0:T(8,128)} %param.10, f32[20,256,512]{2,1,0:T(8,128)} %gather_fusion.3, f32[20,256,512]{2,1,0:T(8,128)} %gather_fusion.2, f32[512]{0:T(512)S(1)} %pad_maximum_fusion), kind=kOutput, calls=%fused_computation.13 | convolution fusion | flops 8056995840 | bytes 31459328 | tf_op jit(solution)/shard_map/sik,sjk->sij/dot_general | solution.py:42
  (36 shorter events, 0.4 us)
Async XLA Ops:
  7.2 65.7 %copy-start = (f32[256,256]{1,0:T(8,128)S(1)}, f32[256,256]{1,0:T(8,128)}, u32[]{:S(2)}) copy-start(f32[256,256]{1,0:T(8,128)} %param.13) | copy-start | bytes 786436
  7.2 130.7 %copy-start.2 = (f32[2,256,512]{2,1,0:T(8,128)S(1)}, f32[2,256,512]{2,1,0:T(8,128)}, u32[]{:S(2)}) copy-start(f32[2,256,512]{2,1,0:T(8,128)} %param.11) | copy-start | bytes 3145732
  7.2 132.5 %copy-start.5 = (s32[128]{0:T(128)S(1)}, s32[128]{0:T(128)}, u32[]{:S(2)}) copy-start(s32[128]{0:T(128)} %param.14) | copy-start | bytes 1540
  7.2 238.1 %all-gather.3.cloned.1.call-start = ((), (), s32[]{:S(2)}) async-start(), calls=%async_computation | async-start | bytes 17039360 | tf_op jit(solution)/shard_map/all_gather | solution.py:58
  45.5 96.2 %copy-start.3 = (s32[64,24]{0,1:T(8,128)S(1)}, s32[64,24]{0,1:T(8,128)}, u32[]{:S(2)}) copy-start(s32[64,24]{0,1:T(8,128)} %param.15) | copy-start | bytes 18436
  141.7 242.7 %all-gather.5.cloned.1.call-start = ((), (), s32[]{:S(2)}) async-start(), calls=%async_computation.1 | async-start | bytes 15728640 | tf_op jit(solution)/shard_map/all_gather | solution.py:61
  141.9 126.7 %copy-start.4 = (s32[20,2]{0,1:T(2,128)S(1)}, s32[20,2]{0,1:T(2,128)}, u32[]{:S(2)}) copy-start(s32[20,2]{0,1:T(2,128)} %param.16) | copy-start | bytes 484
  423.5 38.9 %copy-start.1 = (f32[256,256]{1,0:T(8,128)S(1)}, f32[256,256]{1,0:T(8,128)}, u32[]{:S(2)}) copy-start(f32[256,256]{1,0:T(8,128)} %param.13) | copy-start | bytes 786436
Sparse Core Ops, SparseCore 0:
  141.8 103.4 all-gather.2
  266.9 117.4 all-gather.4
where the time goes:
time: 478 us; the launch traced here: 470 us
  waiting for transfers between devices  219 us (46%)
  other arithmetic  110 us (23%)
  local copies, waits for them, and re-layouts  67.5 us (14%)
  matrix products  55 us (12%)
  between operations  17.5 us (4%)
    all_gather x1, waiting for transfers between devices, per_device(): group_rows = lax.all_gather(selected, 'rep', axis=1, tiled=True)  116 us
    all_gather x1, waiting for transfers between devices, per_device(): lax.all_gather(my_rows, 'tiles', axis=0, tiled=True)  103 us
    another operation x13, other arithmetic, pivot_factor(): lower_factor = jnp.linalg.cholesky(matrix)  68.5 us
    another operation x5, other arithmetic, pivot_factor(): jax.scipy.linalg.solve_triangular(lower_factor, identity, lower=True)  39.8 us
    dot_general x1, matrix products, pair_products(): jnp.einsum('sik,sjk->sij', left_rows, right_rows, precision=lax.Precision...  27.4 us
    dot_general x1, matrix products, per_device(): jnp.einsum('gn,nij->gij', picker, lax.all_gather(my_rows, 'tiles', axis=0...  21.4 us
    all_gather x1, local copies, waits for them, and re-layouts, per_device(): group_rows = lax.all_gather(selected, 'rep', axis=1, tiled=True)  16.4 us
    concatenate x1, local copies, waits for them, and re-layouts, pair_products(): extended = jnp.concatenate([group_rows, padding], axis=0)  11.6 us
  transfers between devices with their start and end apart: 2, of which 2 were waited for; matrix products, arithmetic and copies ran while one was open for 0% of the time, Pallas kernels for 0%

commit v1 on v0

--- a/solution.py
+++ b/solution.py
@@ -43,6 +43,14 @@
 
 
 def per_device(trailing_tiles, panel_rows, pivot_blocks, coupling, row_ids, membership, tile_pairs):
+
+    def point_the_forms(u_in, lane_axis, in_dim):
+        p_next = lax.axis_size(lane_axis)
+        found_now = jnp.stack([u_in] * p_next)
+        opened = lax.all_to_all(found_now, axis_name=lane_axis, split_axis=0, concat_axis=0)
+        fresh = jnp.concatenate(opened, axis=in_dim)
+        return fresh
+
     owned_slots = panel_rows.shape[0]
     panel_width = pivot_blocks.shape[1]
     tile_index = lax.axis_index("tiles")
@@ -53,10 +61,7 @@
     wanted = lax.dynamic_index_in_dim(membership, tile_index, 0, keepdims=False)
     picker = (wanted[:, None] == row_ids[None, :]).astype(jnp.float32)
     selected = jnp.einsum(
-        "gn,nij->gij",
-        picker,
-        lax.all_gather(my_rows, "tiles", axis=0, tiled=True),
-        precision=lax.Precision.HIGHEST,
+        "gn,nij->gij", picker, point_the_forms(my_rows, "tiles", 0), precision=lax.Precision.HIGHEST
     )
     group_rows = lax.all_gather(selected, "rep", axis=1, tiled=True)
     scales = jnp.concatenate([diag_one, diag_two])

time: 478 us -> 792 us (1.66)
  waiting for transfers between devices: 219 us -> 481 us
  local copies, waits for them, and re-layouts: 67.5 us -> 109 us
  starting transfers between devices: 0.08 us -> 13.5 us
  matrix products: 55 us -> 43.9 us
  other arithmetic: 110 us -> 118 us
    all_to_all x0 -> x1, waiting for transfers between devices: none -> 365 us  [point_the_forms(): lax.all_to_all(found_now, axis_name=lane_axis, split_axis=0, concat_axis=0)]
    all_gather x1 -> x0, waiting for transfers between devices: 103 us -> none  [per_device(): lax.all_gather(my_rows, 'tiles', axis=0, tiled=True)]
    reshape x0 -> x1, local copies, waits for them, and re-layouts: none -> 20.5 us  [point_the_forms(): fresh = jnp.concatenate(opened, axis=in_dim)]
    all_to_all x0 -> x1, starting transfers between devices: none -> 13.5 us  [point_the_forms(): lax.all_to_all(found_now, axis_name=lane_axis, split_axis=0, concat_axis=0)]
    all_to_all x0 -> x1, local copies, waits for them, and re-layouts: none -> 12 us  [point_the_forms(): lax.all_to_all(found_now, axis_name=lane_axis, split_axis=0, concat_axis=0)]
    dot_general x1, matrix products: 21.4 us -> 10.3 us  [per_device(): jnp.einsum('gn,nij->gij', picker, point_the_forms(my_rows, 'tiles', 0), p...]
    another operation x0 -> x1, local copies, waits for them, and re-layouts: none -> 9.34 us  [point_the_forms(): found_now = jnp.stack([u_in] * p_next)]
    another operation x5, other arithmetic: 39.8 us -> 47.9 us  [pivot_factor(): jax.scipy.linalg.solve_triangular(lower_factor, identity, lower=True)]
where the time goes in v1:
time: 792 us; the launch traced here: 783 us
  waiting for transfers between devices  481 us (61%)
  other arithmetic  118 us (15%)
  local copies, waits for them, and re-layouts  109 us (14%)
  matrix products  43.9 us (6%)
  between operations  17.5 us (2%)
  starting transfers between devices  13.5 us (2%)
    all_to_all x1, waiting for transfers between devices, point_the_forms(): lax.all_to_all(found_now, axis_name=lane_axis, split_axis=0, concat_axis=0)  365 us
    all_gather x1, waiting for transfers between devices, per_device(): group_rows = lax.all_gather(selected, 'rep', axis=1, tiled=True)  116 us
    another operation x13, other arithmetic, pivot_factor(): lower_factor = jnp.linalg.cholesky(matrix)  68.5 us
    another operation x5, other arithmetic, pivot_factor(): jax.scipy.linalg.solve_triangular(lower_factor, identity, lower=True)  47.9 us
    dot_general x1, matrix products, pair_products(): jnp.einsum('sik,sjk->sij', left_rows, right_rows, precision=lax.Precision...  27.4 us
    reshape x1, local copies, waits for them, and re-layouts, point_the_forms(): fresh = jnp.concatenate(opened, axis=in_dim)  20.5 us
    all_gather x1, local copies, waits for them, and re-layouts, per_device(): group_rows = lax.all_gather(selected, 'rep', axis=1, tiled=True)  16.4 us
  transfers between devices with their start and end apart: 2, of which 2 were waited for; matrix products, arithmetic and copies ran while one was open for 0% of the time, Pallas kernels for 0%

profile of v1, /device:TPU:1, one launch (start us, length us, event | category | flops | bytes accessed | tf_op | source)
XLA Modules:
  0.0 783.1 jit_solution(13617573584774594209)
XLA Ops:
  7.3 1.2 fusion.51
  8.4 0.1 copy.40
  8.6 1.0 fusion.14
  9.6 11.7 %cholesky.130 = f32[128,128]{1,0:T(8,128)S(1)} custom-call(f32[128,128]{1,0:T(8,128)S(1)} %cholesky.194), custom_call_target="Cholesky" | custom-call | tf_op jit(solution)/shard_map/jit(cholesky)/cholesky | solution.py:10
  21.3 9.8 %custom-call.17 = f32[1,128,128]{1,2,0:T(8,128)S(1)} custom-call(f32[1,128,128]{2,1,0:T(8,128)S(1)} %get-tuple-element.63), custom_call_target="InvertDiagBlocksLowerTriangular" | custom-call | tf_op jit(solution)/shard_map/jit(cholesky)/cholesky | solution.py:10
  31.2 0.2 constant_dynamic-update-slice_fusion.3
  31.4 0.3 convolution_subtract_fusion.5
  31.6 11.7 %cholesky.147 = f32[128,128]{1,0:T(8,128)S(1)} custom-call(f32[128,128]{1,0:T(8,128)S(1)} %convolution_subtract_fusion.5), custom_call_target="Cholesky" | custom-call | tf_op jit(solution)/shard_map/jit(cholesky)/cholesky | solution.py:10
  43.4 0.6 compare_reduce_fusion.2
  45.4 0.1 triangular_solve.75
  45.5 4.3 while.4
  45.7 0.6 fusion.67
  46.3 1.4 bitcast_dynamic-update-slice_fusion.4
  47.7 0.6 fusion.67
  48.3 1.4 bitcast_dynamic-update-slice_fusion.4
  49.7 19.7 %custom-call.18 = f32[2,128,128]{1,2,0:T(8,128)S(1)} custom-call(f32[2,128,128]{2,1,0:T(8,128)S(1)} %get-tuple-element.19), custom_call_target="InvertDiagBlocksLowerTriangular" | custom-call | tf_op jit(solution)/shard_map/jit(_solve_triangular)/triangular_solve | solution.py:13
  69.4 0.3 fusion.27
  69.7 0.3 convolution_subtract_fusion.3
  70.0 0.3 fusion.34
  70.3 2.3 gather_fusion
  72.7 0.1 copy.41
  72.8 0.4 fusion.47
  73.3 0.7 convolution_subtract_fusion.1
  73.9 0.1 copy.33
  74.1 11.7 %cholesky.164 = f32[128,128]{1,0:T(8,128)S(1)} custom-call(f32[128,128]{1,0:T(8,128)S(1)} %cholesky.197), custom_call_target="Cholesky" | custom-call | tf_op jit(solution)/shard_map/jit(cholesky)/cholesky | solution.py:10
  85.9 9.8 %custom-call.19 = f32[1,128,128]{1,2,0:T(8,128)S(1)} custom-call(f32[1,128,128]{2,1,0:T(8,128)S(1)} %get-tuple-element.59), custom_call_target="InvertDiagBlocksLowerTriangular" | custom-call | tf_op jit(solution)/shard_map/jit(cholesky)/cholesky | solution.py:10
  95.7 0.2 constant_dynamic-update-slice_fusion.1
  95.9 0.3 convolution_subtract_fusion.4
  96.2 11.7 %cholesky.181 = f32[128,128]{1,0:T(8,128)S(1)} custom-call(f32[128,128]{1,0:T(8,128)S(1)} %convolution_subtract_fusion.4), custom_call_target="Cholesky" | custom-call | tf_op jit(solution)/shard_map/jit(cholesky)/cholesky | solution.py:10
  107.9 0.6 compare_reduce_fusion
  108.6 0.6 compare_reduce_fusion.1
  110.6 4.0 while.5
  110.6 0.6 fusion.68
  111.2 1.4 bitcast_dynamic-update-slice_fusion.5
  112.6 0.6 fusion.68
  113.2 1.4 bitcast_dynamic-update-slice_fusion.5
  114.6 28.1 %custom-call.20 = f32[2,128,128]{1,2,0:T(8,128)S(1)} custom-call(f32[2,128,128]{2,1,0:T(8,128)S(1)} %get-tuple-element.20), custom_call_target="InvertDiagBlocksLowerTriangular" | custom-call | tf_op jit(solution)/shard_map/jit(_solve_triangular)/triangular_solve | solution.py:13
  142.7 0.3 fusion.25
  143.0 0.3 convolution_subtract_fusion.2
  143.3 0.3 fusion.30
  143.6 2.3 gather_fusion.1
  146.0 0.6 convolution_bitcast_fusion
  146.6 1.1 convolution_subtract_fusion
  147.7 0.1 dynamic-slice_compare_fusion
  147.8 0.6 fusion.10
  148.4 0.1 maximum_select_fusion
  148.6 0.2 constant_dynamic-slice_fusion.2
  148.8 0.2 copy.34
  149.0 9.3 %stack.4 = f32[64,2,64,512]{3,1,2,0:T(2,128)} broadcast(f32[2,64,512]{2,0,1:T(2,128)S(1)} %copy.34), dimensions={1,2,3} | broadcast | bytes 17039360 | tf_op jit(solution)/shard_map/stack | solution.py:49
  158.3 13.5 %all-to-all-start = ((f32[64,2,64,512]{3,1,2,0:T(2,128)}), f32[64,2,64,512]{3,1,2,0:T(2,128)}, u32[]{:S(2)}, u32[]{:S(2)}) async-start(f32[64,2,64,512]{3,1,2,0:T(2,128)} %stack.4), calls=%async_computation | async-start | bytes 33554432 | tf_op jit(solution)/shard_map/all_to_all | solution.py:50
  171.8 0.0 all-gather.2.cloned.1.call-start
  171.9 0.2 dynamic-slice_reduce_fusion
  172.1 365.3 %all-to-all-done = f32[64,2,64,512]{3,1,2,0:T(2,128)} async-done(((f32[64,2,64,512]{3,1,2,0:T(2,128)}), f32[64,2,64,512]{3,1,2,0:T(2,128)}, u32[]{:S(2)}, u32[]{:S(2)}) %all-to-all-start) | async-done | bytes 16777248 | tf_op jit(solution)/shard_map/all_to_all | solution.py:50
  537.3 12.0 %copy.35 = f32[64,2,64,512]{3,1,0,2:T(2,128)} copy(f32[64,2,64,512]{3,1,2,0:T(2,128)} %all-to-all-done) | data formatting | bytes 33554432 | tf_op jit(solution)/shard_map/all_to_all | solution.py:50
  549.3 20.5 %reshape.52 = f32[128,64,512]{2,0,1:T(8,128)} reshape(f32[64,2,64,512]{3,1,0,2:T(2,128)} %copy.35) | data formatting | bytes 33554432 | tf_op jit(solution)/shard_map/reshape | solution.py:51
  569.9 10.3 %fusion.39 = f32[24,64,512]{2,0,1:T(8,128)} fusion(f32[128,64,512]{2,0,1:T(8,128)} %reshape.52, s32[128]{0:T(128)S(1)} %copy-done.5, s32[24]{0:T(128)S(1)} %dynamic-slice_reduce_fusion), kind=kOutput, calls=%fused_computation.72 | convolution fusion | flops 1207962624 | bytes 19923552 | tf_op jit(solution)/shard_map/gn,nij->gij/dot_general | solution.py:63
  580.3 1.3 copy.37
  581.6 0.6 pad_maximum_fusion.1
  582.2 115.6 %all-gather.2.cloned.1.call-done = f32[24,256,512]{2,0,1:T(8,128)} async-done(((f32[24,64,512]{2,0,1:T(8,128)}), f32[24,256,512]{2,0,1:T(8,128)}) %all-gather.2.cloned.1.call-update) | async-done | bytes 12582928 | tf_op jit(solution)/shard_map/all_gather | solution.py:66
  697.8 16.4 %copy.36 = f32[24,256,512]{2,1,0:T(8,128)} copy(f32[24,256,512]{2,0,1:T(8,128)} %all-gather.2.cloned.1.call-done) | data formatting | bytes 25165824 | tf_op jit(solution)/shard_map/all_gather | solution.py:66
  714.2 11.6 %concatenate.18 = f32[25,256,512]{2,1,0:T(8,128)} pad(f32[24,256,512]{2,1,0:T(8,128)} %copy.36, f32[]{:T(128)} %constant.92.clone.1), padding=0_1x0_0x0_0 | pad | bytes 25690116 | tf_op jit(solution)/shard_map/concatenate | solution.py:39
  725.8 11.2 %gather_fusion.2 = f32[20,256,512]{2,1,0:T(8,128)} fusion(f32[25,256,512]{2,1,0:T(8,128)} %concatenate.18, s32[1024]{0:T(1024)S(1)} %get-tuple-element.73), kind=kCustom, calls=%fused_computation.2 | custom fusion | bytes 20971600 | tf_op jit(solution)/shard_map/gather | solution.py:40
  736.9 11.5 %gather_fusion.3 = f32[20,256,512]{2,1,0:T(8,128)} fusion(f32[25,256,512]{2,1,0:T(8,128)} %concatenate.18, s32[1024]{0:T(1024)S(1)} %get-tuple-element.72), kind=kCustom, calls=%fused_computation.3 | custom fusion | bytes 20971600 | tf_op jit(solution)/shard_map/gather | solution.py:41
  748.4 27.4 %fusion.3 = f32[20,256,256]{2,1,0:T(8,128)} fusion(f32[20,256,256]{2,1,0:T(8,128)} %param.10, f32[20,256,512]{2,1,0:T(8,128)} %gather_fusion.3, f32[20,256,512]{2,1,0:T(8,128)} %gather_fusion.2, f32[512]{0:T(512)S(1)} %pad_maximum_fusion), kind=kOutput, calls=%fused_computation.11 | convolution fusion | flops 8056995840 | bytes 31459328 | tf_op jit(solution)/shard_map/sik,sjk->sij/dot_general | solution.py:42
  (38 shorter events, 0.5 us)
Async XLA Ops:
  7.2 65.7 %copy-start = (f32[256,256]{1,0:T(8,128)S(1)}, f32[256,256]{1,0:T(8,128)}, u32[]{:S(2)}) copy-start(f32[256,256]{1,0:T(8,128)} %param.13) | copy-start | bytes 786436
  7.2 138.8 %copy-start.2 = (f32[2,256,512]{2,1,0:T(8,128)S(1)}, f32[2,256,512]{2,1,0:T(8,128)}, u32[]{:S(2)}) copy-start(f32[2,256,512]{2,1,0:T(8,128)} %param.11) | copy-start | bytes 3145732
  7.2 140.5 %copy-start.5 = (s32[128]{0:T(128)S(1)}, s32[128]{0:T(128)}, u32[]{:S(2)}) copy-start(s32[128]{0:T(128)} %param.14) | copy-start | bytes 1540
  158.3 13.5 %copy-start.3 = (s32[64,24]{0,1:T(8,128)S(1)}, s32[64,24]{0,1:T(8,128)}, u32[]{:S(2)}) copy-start(s32[64,24]{0,1:T(8,128)} %param.15) | copy-start | bytes 18436
  158.3 379.0 %all-to-all-start = ((f32[64,2,64,512]{3,1,2,0:T(2,128)}), f32[64,2,64,512]{3,1,2,0:T(2,128)}, u32[]{:S(2)}, u32[]{:S(2)}) async-start(f32[64,2,64,512]{3,1,2,0:T(2,128)} %stack.4), calls=%async_computation | async-start | bytes 33554432 | tf_op jit(solution)/shard_map/all_to_all | solution.py:50
  171.8 526.0 %all-gather.2.cloned.1.call-start = ((), (), s32[]{:S(2)}) async-start(), calls=%async_computation.1 | async-start | bytes 15728640 | tf_op jit(solution)/shard_map/all_gather | solution.py:66
  569.9 12.3 %copy-start.4 = (s32[20,2]{0,1:T(2,128)S(1)}, s32[20,2]{0,1:T(2,128)}, u32[]{:S(2)}) copy-start(s32[20,2]{0,1:T(2,128)} %param.16) | copy-start | bytes 484
  736.9 38.9 %copy-start.1 = (f32[256,256]{1,0:T(8,128)S(1)}, f32[256,256]{1,0:T(8,128)}, u32[]{:S(2)}) copy-start(f32[256,256]{1,0:T(8,128)} %param.13) | copy-start | bytes 786436
Sparse Core Ops, SparseCore 0:
  580.4 117.3 all-gather.1
